TPU v7x, 32 devices: a whole 2x2x4 slice. The times are simulated.
32 devices in a mesh: dp: 16 (over z, y, core), query: 2 (over x).
Axes of the slice: x: 2, y: 2, z: 4, core: 2. Of those that a mesh axis runs over, the one named last changes fastest.
Arguments:
- tokens: bfloat16 [2, 32, 128, 1280], P(None, ('dp', 'query')), may hold values from -6 to 6
- out_cotangent: bfloat16 [2, 32, 128, 1280], P(None, ('dp', 'query')), may hold values from -6 to 6
- qkv_weight: bfloat16 [1280, 3840], P('dp'), may hold values from -0.15625 to 0.15625
- out_weight: bfloat16 [1280, 1280], P('dp'), may hold values from -0.625 to 0.625
- up_weight: bfloat16 [1280, 5120], P('dp'), may hold values from -0.15625 to 0.15625
- down_weight: bfloat16 [5120, 1280], P('dp'), may hold values from -0.078125 to 0.078125
- attn_gain: bfloat16 [1280], P('dp'), may hold values from 0.5 to 1.5
- ffn_gain: bfloat16 [1280], P('dp'), may hold values from 0.5 to 1.5
- up_bias: bfloat16 [5120], P('dp'), may hold values from -3 to 3
- cell_weight: bfloat16 [1280, 5120], P('dp'), may hold values from -0.15625 to 0.15625
- gene_weight: bfloat16 [1280, 5120], P('dp'), may hold values from -0.15625 to 0.15625
- decoder_bias: bfloat16 [5120], P('dp'), may hold values from -3 to 3
- readout: bfloat16 [5120], P('dp'), may hold values from -0.15625 to 0.15625
- gene_embed: bfloat16 [2, 32, 384, 1280], P(None, ('dp', 'query')), may hold values from -6 to 6
- query_cell: int32 [2, 32, 384], P(None, ('dp', 'query')), may hold values from 0 to 1
- query_label: int32 [2, 32, 384], P(None, ('dp', 'query')), may hold values 0 or 1
- query_live: int32 [16, 2, 2], P('dp', None, 'query'), may hold values from 1 to 384, 480 in all within a row
Outputs:
- block_out: bfloat16 [2, 32, 128, 1280], P(None, ('dp', 'query'))
- grad_tokens: float32 [2, 32, 128, 1280], P(None, ('dp', 'query'))
- grad_qkv: float32 [1280, 3840], P('dp')
- grad_out: float32 [1280, 1280], P('dp')
- grad_up: float32 [1280, 5120], P('dp')
- grad_down: float32 [5120, 1280], P('dp')
- grad_attn_gain: float32 [1280], P('dp')
- grad_ffn_gain: float32 [1280], P('dp')
- grad_up_bias: float32 [5120], P('dp')
- grad_cell: float32 [1280, 5120], P('dp')
- grad_gene: float32 [1280, 5120], P('dp')
- grad_decoder_bias: float32 [5120], P('dp')
- grad_readout: float32 [5120], P('dp')
Inputs may be any that keep to these rules, and one draw needn't show every extreme that they name: `query_live`: the 2 devices of one dp index together hold 480 live rows in each micro-batch; a device's live rows are its first slots. `query_cell`: index of a cell within the query group of the row's device.
All inputs are finite; a program needn't handle non-finite values. No bound on the sum of `query_label` on one device may be relied on, other than what follows from the above.
Results may differ from a plain program's by a relative error of at most 0.02.
Values may be sent and summed in bfloat16 or wider, within the bound.
No kernel may reach another device: no remote copies, remote signals or barrier semaphores. Data moves between devices by JAX's collectives and lax.ppermute only.
A program may use at most 320 MiB of HBM per device.

v0:
```python
import jax
import jax.numpy as jnp
from jax import lax
from jax.sharding import PartitionSpec as P

D = 1280
HEADS = 20
HEAD = 64
highest = lax.Precision.HIGHEST
epsilon = 1e-05


def row_product(left, right):
    return lax.dot_general(
        left, right, (((0,), (0,)), ((), ())), preferred_element_type=jnp.float32
    )


def times_transpose(left, right):
    return lax.dot_general(
        left, right, (((1,), (1,)), ((), ())), preferred_element_type=jnp.float32
    )


def layer_stats(values):
    average = jnp.mean(values, axis=-1, keepdims=True)
    centred = values - average
    variance = jnp.mean(centred * centred, axis=-1, keepdims=True)
    inverse = lax.rsqrt(variance + epsilon)
    return (centred * inverse, inverse)


def norm_back(grad_scaled, gain, normal, inverse):
    grad_normal = grad_scaled * gain
    along_normal = jnp.mean(grad_normal * normal, axis=-1, keepdims=True)
    average = jnp.mean(grad_normal, axis=-1, keepdims=True)
    grad_values = inverse * (grad_normal - average - normal * along_normal)
    return (grad_values, jnp.sum(grad_scaled * normal, axis=0))


def encode(inputs, weights):
    qkv_weight, out_weight, up_weight, down_weight, attn_gain, ffn_gain, up_bias = weights
    length = inputs.shape[0]
    tokens_wide = inputs.astype(jnp.float32)
    norm_one, scale_one = layer_stats(tokens_wide)
    normed = (norm_one * attn_gain.astype(jnp.float32)).astype(jnp.bfloat16)
    projected = jnp.dot(normed, qkv_weight, preferred_element_type=jnp.float32).astype(jnp.bfloat16)
    projected = projected.reshape(length, 3, HEADS, HEAD)
    queries = projected[:, 0]
    key_heads = projected[:, 1]
    value_heads = projected[:, 2]
    scores = (
        jnp.einsum("qhd,khd->hqk", queries, key_heads, preferred_element_type=jnp.float32) * 0.125
    )
    row_max = jnp.max(scores, axis=-1, keepdims=True)
    shifted = jnp.exp(scores - row_max)
    row_total = jnp.sum(shifted, axis=-1, keepdims=True)
    attn_probs = (shifted / row_total).astype(jnp.bfloat16)
    logsum = row_max + jnp.log(row_total)
    mixed_heads = jnp.einsum(
        "hqk,khd->qhd", attn_probs, value_heads, preferred_element_type=jnp.float32
    )
    mixed_heads = mixed_heads.astype(jnp.bfloat16).reshape(length, D)
    hidden = tokens_wide + jnp.dot(mixed_heads, out_weight, preferred_element_type=jnp.float32)
    norm_two, scale_two = layer_stats(hidden)
    second = (norm_two * ffn_gain.astype(jnp.float32)).astype(jnp.bfloat16)
    up_proj = jnp.dot(second, up_weight, preferred_element_type=jnp.float32) + up_bias.astype(
        jnp.float32
    )
    active = jax.nn.gelu(up_proj, approximate=True).astype(jnp.bfloat16)
    output = hidden + jnp.dot(active, down_weight, preferred_element_type=jnp.float32)
    saved_state = (
        norm_one,
        scale_one,
        normed,
        queries,
        key_heads,
        value_heads,
        logsum,
        mixed_heads,
        norm_two,
        scale_two,
        second,
        up_proj,
        active,
    )
    return (output, saved_state)


def encode_back(grad_output, saved_state, weights):
    qkv_weight, out_weight, up_weight, down_weight, attn_gain, ffn_gain = weights
    (
        norm_one,
        scale_one,
        normed,
        queries,
        key_heads,
        value_heads,
        logsum,
        mixed_heads,
        norm_two,
        scale_two,
        second,
        up_proj,
        active,
    ) = saved_state
    length = grad_output.shape[0]
    grad_branch = grad_output.astype(jnp.bfloat16)
    grad_down = row_product(active, grad_branch)
    grad_active = times_transpose(grad_branch, down_weight)
    gelu_back = jax.vjp(lambda inner_values: jax.nn.gelu(inner_values, approximate=True), up_proj)[
        1
    ]
    grad_up_proj = gelu_back(grad_active)[0].astype(jnp.bfloat16)
    grad_up = row_product(second, grad_up_proj)
    grad_up_bias = jnp.sum(grad_up_proj.astype(jnp.float32), axis=0)
    grad_second = times_transpose(grad_up_proj, up_weight)
    grad_hidden_norm, grad_ffn_gain = norm_back(
        grad_second, ffn_gain.astype(jnp.float32), norm_two, scale_two
    )
    grad_hidden = grad_output + grad_hidden_norm
    grad_attn = grad_hidden.astype(jnp.bfloat16)
    grad_out = row_product(mixed_heads, grad_attn)
    grad_mixed = (
        times_transpose(grad_attn, out_weight).astype(jnp.bfloat16).reshape(length, HEADS, HEAD)
    )
    scores = (
        jnp.einsum("qhd,khd->hqk", queries, key_heads, preferred_element_type=jnp.float32) * 0.125
    )
    attn_probs = jnp.exp(scores - logsum)
    probs_low = attn_probs.astype(jnp.bfloat16)
    grad_values = jnp.einsum(
        "hqk,qhd->khd", probs_low, grad_mixed, preferred_element_type=jnp.float32
    )
    grad_probs = jnp.einsum(
        "qhd,khd->hqk", grad_mixed, value_heads, preferred_element_type=jnp.float32
    )
    along_probs = jnp.sum(grad_probs * attn_probs, axis=-1, keepdims=True)
    grad_scores = (attn_probs * (grad_probs - along_probs) * 0.125).astype(jnp.bfloat16)
    grad_queries = jnp.einsum(
        "hqk,khd->qhd", grad_scores, key_heads, preferred_element_type=jnp.float32
    )
    grad_keys = jnp.einsum("hqk,qhd->khd", grad_scores, queries, preferred_element_type=jnp.float32)
    grad_projected = (
        jnp.stack([grad_queries, grad_keys, grad_values], axis=1)
        .astype(jnp.bfloat16)
        .reshape(length, 3 * D)
    )
    grad_qkv = row_product(normed, grad_projected)
    grad_normed = times_transpose(grad_projected, qkv_weight)
    grad_input_norm, grad_attn_gain = norm_back(
        grad_normed, attn_gain.astype(jnp.float32), norm_one, scale_one
    )
    grad_input = grad_hidden + grad_input_norm
    return (
        (grad_qkv, grad_out, grad_up, grad_down, grad_attn_gain, grad_ffn_gain, grad_up_bias),
        grad_input,
    )


def decode(summary_all, weights, gene_rows, cell_ids, labels, live_count):
    cell_weight, gene_weight, decoder_bias, readout = weights
    group_size = summary_all.shape[0]
    slot_count = gene_rows.shape[0]
    cell_part = jnp.dot(summary_all, cell_weight, preferred_element_type=jnp.float32)
    onehot = (cell_ids[:, None] == jnp.arange(group_size, dtype=jnp.int32)[None, :]).astype(
        jnp.float32
    )
    picked = jnp.dot(onehot, cell_part, precision=highest)
    pre_act = (
        picked
        + jnp.dot(gene_rows, gene_weight, preferred_element_type=jnp.float32)
        + decoder_bias.astype(jnp.float32)
    )
    activity, silu_back = jax.vjp(jax.nn.silu, pre_act)
    read_wide = readout.astype(jnp.float32)
    logits = jnp.sum(activity * read_wide[None, :], axis=-1)
    live_rows = (jnp.arange(slot_count, dtype=jnp.int32) < live_count).astype(jnp.float32)
    grad_logits = live_rows * (jax.nn.sigmoid(logits) - labels.astype(jnp.float32))
    grad_readout = jnp.sum(grad_logits[:, None] * activity, axis=0)
    grad_pre = silu_back(grad_logits[:, None] * read_wide[None, :])[0].astype(jnp.bfloat16)
    grad_pre_wide = grad_pre.astype(jnp.float32)
    grad_decoder_bias = jnp.sum(grad_pre_wide, axis=0)
    grad_gene = row_product(gene_rows, grad_pre)
    grad_cellproj = lax.dot_general(
        onehot, grad_pre_wide, (((0,), (0,)), ((), ())), precision=highest
    )
    grad_cell = lax.dot_general(
        summary_all.astype(jnp.float32), grad_cellproj, (((0,), (0,)), ((), ())), precision=highest
    )
    grad_summary = lax.dot_general(
        grad_cellproj, cell_weight.astype(jnp.float32), (((1,), (1,)), ((), ())), precision=highest
    )
    return ((grad_cell, grad_gene, grad_decoder_bias, grad_readout), grad_summary)


def shards(
    tokens,
    out_cotangent,
    qkv_weight,
    out_weight,
    up_weight,
    down_weight,
    attn_gain,
    ffn_gain,
    up_bias,
    cell_weight,
    gene_weight,
    decoder_bias,
    readout,
    gene_embed,
    query_cell,
    query_label,
    query_live,
):
    micro_count = tokens.shape[0]
    outputs = []
    input_grads = []
    totals = None
    for micro_index in range(micro_count):
        gathered = (
            lax.all_gather(qkv_weight, "dp", axis=0, tiled=True),
            lax.all_gather(out_weight, "dp", axis=0, tiled=True),
            lax.all_gather(up_weight, "dp", axis=0, tiled=True),
            lax.all_gather(down_weight, "dp", axis=0, tiled=True),
            lax.all_gather(attn_gain, "dp", axis=0, tiled=True),
            lax.all_gather(ffn_gain, "dp", axis=0, tiled=True),
            lax.all_gather(up_bias, "dp", axis=0, tiled=True),
            lax.all_gather(cell_weight, "dp", axis=0, tiled=True),
            lax.all_gather(gene_weight, "dp", axis=0, tiled=True),
            lax.all_gather(decoder_bias, "dp", axis=0, tiled=True),
            lax.all_gather(readout, "dp", axis=0, tiled=True),
        )
        output, saved_state = encode(tokens[micro_index, 0], gathered[:7])
        outputs.append(output.astype(jnp.bfloat16))
        summary_all = lax.all_gather(output[0:1].astype(jnp.bfloat16), "query", axis=0, tiled=True)
        decoder_grads, grad_summary = decode(
            summary_all,
            gathered[7:],
            gene_embed[micro_index, 0],
            query_cell[micro_index, 0],
            query_label[micro_index, 0],
            query_live[0, micro_index, 0],
        )
        grad_own = lax.psum_scatter(
            grad_summary.astype(jnp.bfloat16), "query", scatter_dimension=0, tiled=True
        ).astype(jnp.float32)
        grad_output = out_cotangent[micro_index, 0].astype(jnp.float32)
        grad_output = grad_output.at[0:1].add(grad_own)
        back_weights = (
            lax.all_gather(qkv_weight, "dp", axis=0, tiled=True),
            lax.all_gather(out_weight, "dp", axis=0, tiled=True),
            lax.all_gather(up_weight, "dp", axis=0, tiled=True),
            lax.all_gather(down_weight, "dp", axis=0, tiled=True),
            lax.all_gather(attn_gain, "dp", axis=0, tiled=True),
            lax.all_gather(ffn_gain, "dp", axis=0, tiled=True),
        )
        encoder_grads, grad_input = encode_back(grad_output, saved_state, back_weights)
        input_grads.append(grad_input)
        step_grads = encoder_grads + decoder_grads
        if micro_index == 0:
            totals = tuple(step_grads)
        else:
            totals = tuple((earlier + later for earlier, later in zip(totals, step_grads)))
    owned = (
        lax.psum_scatter(
            totals[0].astype(jnp.bfloat16), "dp", scatter_dimension=0, tiled=True
        ).astype(jnp.float32),
        lax.psum_scatter(
            totals[1].astype(jnp.bfloat16), "dp", scatter_dimension=0, tiled=True
        ).astype(jnp.float32),
        lax.psum_scatter(
            totals[2].astype(jnp.bfloat16), "dp", scatter_dimension=0, tiled=True
        ).astype(jnp.float32),
        lax.psum_scatter(
            totals[3].astype(jnp.bfloat16), "dp", scatter_dimension=0, tiled=True
        ).astype(jnp.float32),
        lax.psum_scatter(
            totals[4].astype(jnp.bfloat16), "dp", scatter_dimension=0, tiled=True
        ).astype(jnp.float32),
        lax.psum_scatter(
            totals[5].astype(jnp.bfloat16), "dp", scatter_dimension=0, tiled=True
        ).astype(jnp.float32),
        lax.psum_scatter(
            totals[6].astype(jnp.bfloat16), "dp", scatter_dimension=0, tiled=True
        ).astype(jnp.float32),
        lax.psum_scatter(
            totals[7].astype(jnp.bfloat16), "dp", scatter_dimension=0, tiled=True
        ).astype(jnp.float32),
        lax.psum_scatter(
            totals[8].astype(jnp.bfloat16), "dp", scatter_dimension=0, tiled=True
        ).astype(jnp.float32),
        lax.psum_scatter(
            totals[9].astype(jnp.bfloat16), "dp", scatter_dimension=0, tiled=True
        ).astype(jnp.float32),
        lax.psum_scatter(
            totals[10].astype(jnp.bfloat16), "dp", scatter_dimension=0, tiled=True
        ).astype(jnp.float32),
    )
    totals = (
        lax.psum(owned[0].astype(jnp.bfloat16), "query").astype(jnp.float32),
        lax.psum(owned[1].astype(jnp.bfloat16), "query").astype(jnp.float32),
        lax.psum(owned[2].astype(jnp.bfloat16), "query").astype(jnp.float32),
        lax.psum(owned[3].astype(jnp.bfloat16), "query").astype(jnp.float32),
        lax.psum(owned[4].astype(jnp.bfloat16), "query").astype(jnp.float32),
        lax.psum(owned[5].astype(jnp.bfloat16), "query").astype(jnp.float32),
        lax.psum(owned[6].astype(jnp.bfloat16), "query").astype(jnp.float32),
        lax.psum(owned[7].astype(jnp.bfloat16), "query").astype(jnp.float32),
        lax.psum(owned[8].astype(jnp.bfloat16), "query").astype(jnp.float32),
        lax.psum(owned[9].astype(jnp.bfloat16), "query").astype(jnp.float32),
        lax.psum(owned[10].astype(jnp.bfloat16), "query").astype(jnp.float32),
    )
    block_out = jnp.stack(outputs, axis=0)[:, None]
    grad_tokens = jnp.stack(input_grads, axis=0)[:, None]
    return (
        block_out,
        grad_tokens,
        totals[0],
        totals[1],
        totals[2],
        totals[3],
        totals[4],
        totals[5],
        totals[6],
        totals[7],
        totals[8],
        totals[9],
        totals[10],
    )


def solution(mesh):
    placed = (
        P(None, ("dp", "query"), None, None),
        P(None, ("dp", "query"), None, None),
        P("dp", None),
        P("dp", None),
        P("dp", None),
        P("dp", None),
        P("dp"),
        P("dp"),
        P("dp"),
        P("dp", None),
        P("dp", None),
        P("dp"),
        P("dp"),
        P(None, ("dp", "query"), None, None),
        P(None, ("dp", "query"), None),
        P(None, ("dp", "query"), None),
        P("dp", None, "query"),
    )
    return jax.shard_map(
        shards,
        mesh=mesh,
        in_specs=placed,
        out_specs=(
            P(None, ("dp", "query"), None, None),
            P(None, ("dp", "query"), None, None),
            P("dp", None),
            P("dp", None),
            P("dp", None),
            P("dp", None),
            P("dp"),
            P("dp"),
            P("dp"),
            P("dp", None),
            P("dp", None),
            P("dp"),
            P("dp"),
        ),
        check_vma=False,
    )
```

profile of v0, /device:TPU:0, one launch (start us, length us, event | category | flops | bytes accessed | tf_op | source)
XLA Modules:
  0.0 1549.0 jit_solution(1948422574728645002)
XLA Ops:
  14.5 65.3 %all-reduce.13 = (bf16[1280]{0:T(1024)(128)(2,1)S(1)}, bf16[5120]{0:T(1024)(128)(2,1)S(1)}, bf16[1280]{0:T(1024)(128)(2,1)S(1)}, bf16[5120]{0:T(1024)(128)(2,1)S(1)}, bf16[5120]{0:T(1024)(128)(2,1)S(1)}) all-reduce(bf16[1280]{0:T(1024)(128)(2,1)S(1)} %dynamic-update-slice.6, ...), channel_id=1, replica_groups=mesh['dp'=16,'query'=2] {'dp'}, use_global_device_ids=true, to_apply=%add | all-reduce | flops 17920 | bytes 71680
  81.0 16.6 %all-gather.9.cloned.1.call-done = bf16[1280,3840]{1,0:T(8,128)(2,1)} async-done(((bf16[80,3840]{1,0:T(8,128)(2,1)}), bf16[1280,3840]{1,0:T(8,128)(2,1)}) %all-gather.9.cloned.1.call-update) | async-done | bytes 9830416 | tf_op jit(solution)/shard_map/all_gather | solution.py:222
  112.9 31.2 %all-gather.11.cloned.1.call-done = bf16[1280,1280]{1,0:T(8,128)(2,1)} async-done(((bf16[80,1280]{1,0:T(8,128)(2,1)}), bf16[1280,1280]{1,0:T(8,128)(2,1)}) %all-gather.11.cloned.1.call-update) | async-done | bytes 3276816 | tf_op jit(solution)/shard_map/all_gather | solution.py:223
  151.0 98.3 %all-gather.13.cloned.1.call-done = bf16[1280,5120]{1,0:T(8,128)(2,1)} async-done(((bf16[80,5120]{1,0:T(8,128)(2,1)}), bf16[1280,5120]{1,0:T(8,128)(2,1)}) %all-gather.13.cloned.1.call-update) | async-done | bytes 13107216 | tf_op jit(solution)/shard_map/all_gather | solution.py:224
  257.5 96.1 %all-gather.15.cloned.1.call-done = bf16[5120,1280]{1,0:T(8,128)(2,1)} async-done(((bf16[320,1280]{1,0:T(8,128)(2,1)}), bf16[5120,1280]{1,0:T(8,128)(2,1)}) %all-gather.15.cloned.1.call-update) | async-done | bytes 13107216 | tf_op jit(solution)/shard_map/all_gather | solution.py:225
  375.1 82.8 %all-gather.17.cloned.1.call-done = bf16[1280,5120]{1,0:T(8,128)(2,1)} async-done(((bf16[80,5120]{1,0:T(8,128)(2,1)}), bf16[1280,5120]{1,0:T(8,128)(2,1)}) %all-gather.17.cloned.1.call-update) | async-done | bytes 13107216 | tf_op jit(solution)/shard_map/all_gather | solution.py:229
  464.5 97.8 %all-gather.19.cloned.1.call-done = bf16[1280,5120]{1,0:T(8,128)(2,1)} async-done(((bf16[80,5120]{1,0:T(8,128)(2,1)}), bf16[1280,5120]{1,0:T(8,128)(2,1)}) %all-gather.19.cloned.1.call-update) | async-done | bytes 13107216 | tf_op jit(solution)/shard_map/all_gather | solution.py:230
  615.9 12.7 fusion.51
  628.6 16.2 %fusion.2 = bf16[1280,5120]{0,1:T(8,128)(2,1)} fusion(f32[5120,1280]{1,0:T(8,128)} %fusion.51, bf16[384,5120]{1,0:T(8,128)(2,1)} %get-tuple-element.137, bf16[2,1,384,1280]{3,2,1,0:T(8,128)(2,1)} %param.34), kind=kOutput, calls=%fused_computation.7 | convolution fusion | flops 5046272000 | bytes 44236800 | tf_op jit(solution)/shard_map/dot_general | solution.py:14
  644.8 17.6 %copy.89 = bf16[1280,5120]{1,0:T(8,128)(2,1)} copy(bf16[1280,5120]{0,1:T(8,128)(2,1)} %fusion.2) | data formatting | bytes 26214400
  670.4 14.2 convolution_convert_fusion.5
  684.5 13.5 convolution_convert_fusion.4
  806.7 12.7 fusion.185
  819.5 15.7 %add_convert_fusion.3 = bf16[1280,5120]{1,0:T(8,128)(2,1)} fusion(f32[1280,5120]{1,0:T(8,128)} %fusion.185, bf16[128,5120]{1,0:T(8,128)(2,1)} %copy-done.26, f32[128,1280]{1,0:T(8,128)S(1)} %copy-done.6, f32[128]{0:T(128)S(1)} %copy-done.75, f32[128]{0:T(128)S(1)} %copy-done.70, f32[1280]{0:T(1024)S(1)} %convert_element_type.331), kind=kOutput, calls=%fused_computation.5 | convolution fusion | flops 1691484160 | bytes 41293824 | tf_op jit(solution)/shard_map/dot_general | solution.py:14
  836.3 12.8 fusion.146
  849.1 16.3 %add_convert_fusion.2 = bf16[5120,1280]{1,0:T(8,128)(2,1)} fusion(f32[5120,1280]{1,0:T(8,128)} %fusion.146, f32[128,1280]{1,0:T(8,128)S(1)} %copy-done.22, f32[128,5120]{1,0:T(8,128)} %convolution_add_fusion.1), kind=kOutput, calls=%fused_computation.4 | convolution fusion | flops 1696890880 | bytes 42598400 | tf_op jit(solution)/shard_map/dot_general | solution.py:14
  866.1 13.9 fusion.167
  880.0 19.8 %add_convert_fusion.1 = bf16[1280,5120]{1,0:T(8,128)(2,1)} fusion(f32[1280,5120]{1,0:T(8,128)} %fusion.167, f32[2,5120]{1,0:T(2,128)S(1)} %fusion.134, bf16[2,1,1280]{2,1,0:T(2,128)(2,1)S(1)} %copy-done.61), kind=kOutput, calls=%fused_computation.3 | convolution fusion | flops 170393600 | bytes 39367680 | tf_op jit(solution)/shard_map/dot_general | solution.py:188
  903.5 83.3 %reduce-scatter.9.cloned.1.call-done = bf16[80,3840]{1,0:T(8,128)(2,1)} async-done(((bf16[1280,3840]{1,0:T(8,128)(2,1)}), bf16[80,3840]{1,0:T(8,128)(2,1)}) %reduce-scatter.9.cloned.1.call-update) | async-done | bytes 614416 | tf_op jit(solution)/shard_map/reduce_scatter | solution.py:266
  986.8 142.1 %reduce-scatter.13.cloned.1.call-done = bf16[80,5120]{1,0:T(8,128)(2,1)} async-done(((bf16[1280,5120]{1,0:T(8,128)(2,1)}), bf16[80,5120]{1,0:T(8,128)(2,1)}) %reduce-scatter.13.cloned.1.call-update) | async-done | bytes 819216 | tf_op jit(solution)/shard_map/reduce_scatter | solution.py:272
  1128.9 142.2 %reduce-scatter.15.cloned.1.call-done = bf16[320,1280]{1,0:T(8,128)(2,1)} async-done(((bf16[5120,1280]{1,0:T(8,128)(2,1)}), bf16[320,1280]{1,0:T(8,128)(2,1)}) %reduce-scatter.15.cloned.1.call-update) | async-done | bytes 819216 | tf_op jit(solution)/shard_map/reduce_scatter | solution.py:275
  1271.1 141.5 %reduce-scatter.17.cloned.1.call-done = bf16[80,5120]{1,0:T(8,128)(2,1)} async-done(((bf16[1280,5120]{1,0:T(8,128)(2,1)}), bf16[80,5120]{1,0:T(8,128)(2,1)}) %reduce-scatter.17.cloned.1.call-update) | async-done | bytes 819216 | tf_op jit(solution)/shard_map/reduce_scatter | solution.py:287
  1428.5 59.6 %all-reduce.12 = (bf16[1280]{0:T(1024)(128)(2,1)S(1)}, bf16[1280]{0:T(1024)(128)(2,1)S(1)}, bf16[5120]{0:T(1024)(128)(2,1)S(1)}, bf16[5120]{0:T(1024)(128)(2,1)S(1)}, bf16[5120]{0:T(1024)(128)(2,1)S(1)}) all-reduce(bf16[1280]{0:T(1024)(128)(2,1)S(1)} %add_convert_fusion.9, ...), channel_id=8, replica_groups=mesh['dp'=16,'query'=2] {'dp'}, use_global_device_ids=true, to_apply=%region_36.37.clone | all-reduce | flops 17920 | bytes 71680
  1499.9 33.9 %all-reduce.19.cloned.1.call-done = (bf16[80,5120]{0,1:T(8,128)(2,1)}, bf16[80,3840]{1,0:T(8,128)(2,1)}, bf16[80,1280]{1,0:T(8,128)(2,1)}, bf16[80,5120]{1,0:T(8...) async-done(((bf16[80,5120]{0,1:T(8,128)(2,1)}, bf16[80,3840]{1,0:T(8,128)(2,1)}, bf16[80,1280]{1,0:T(8,128)(2,1)}, bf16[80,5120]{1,0:T(8,128)(2,1)}, ...) | async-done | bytes 4096016 | tf_op jit(solution)/shard_map/psum | solution.py:309
  (359 shorter events, 275.0 us)
Async XLA Ops:
  7.3 90.3 %all-gather.9.cloned.1.call-start = ((), (), s32[]{:S(2)}) async-start(), calls=%async_computation.6 | async-start | bytes 10444800 | tf_op jit(solution)/shard_map/all_gather | solution.py:222
  8.0 136.1 %all-gather.11.cloned.1.call-start = ((), (), s32[]{:S(2)}) async-start(), calls=%async_computation.7 | async-start | bytes 3481600 | tf_op jit(solution)/shard_map/all_gather | solution.py:223
  8.8 240.5 %all-gather.13.cloned.1.call-start = ((), (), s32[]{:S(2)}) async-start(), calls=%async_computation.8 | async-start | bytes 13926400 | tf_op jit(solution)/shard_map/all_gather | solution.py:224
  9.5 344.1 %all-gather.15.cloned.1.call-start = ((), (), s32[]{:S(2)}) async-start(), calls=%async_computation.9 | async-start | bytes 13926400 | tf_op jit(solution)/shard_map/all_gather | solution.py:225
  10.1 447.9 %all-gather.17.cloned.1.call-start = ((), (), s32[]{:S(2)}) async-start(), calls=%async_computation.10 | async-start | bytes 13926400 | tf_op jit(solution)/shard_map/all_gather | solution.py:229
  10.7 551.6 %all-gather.19.cloned.1.call-start = ((), (), s32[]{:S(2)}) async-start(), calls=%async_computation.11 | async-start | bytes 13926400 | tf_op jit(solution)/shard_map/all_gather | solution.py:230
  11.2 889.9 %reduce-scatter.19.cloned.1.call-start = ((), (), s32[]{:S(2)}) async-start(), calls=%async_computation.17 | async-start | bytes 13926400
  146.8 605.1 %copy-start.5 = (f32[128,1280]{1,0:T(8,128)}, f32[128,1280]{1,0:T(8,128)S(1)}, u32[]{:S(2)}) copy-start(f32[128,1280]{1,0:T(8,128)S(1)} %get-tuple-element.146) | copy-start | bytes 1966084
  146.8 102.5 %copy-start.69 = (f32[128]{0:T(128)}, f32[128]{0:T(128)S(1)}, u32[]{:S(2)}) copy-start(f32[128]{0:T(128)S(1)} %broadcast_multiply_fusion.8) | copy-start | bytes 1540
  150.7 589.7 %copy-start.9 = (f32[128,1280]{1,0:T(8,128)}, f32[128,1280]{1,0:T(8,128)S(1)}, u32[]{:S(2)}) copy-start(f32[128,1280]{1,0:T(8,128)S(1)} %get-tuple-element.150) | copy-start | bytes 1966084
  151.0 106.5 %copy-start.74 = (f32[128]{0:T(128)}, f32[128]{0:T(128)S(1)}, u32[]{:S(2)}) copy-start(f32[128]{0:T(128)S(1)} %add_rsqrt_fusion) | copy-start | bytes 1540
  366.3 91.6 %copy-start.60 = (bf16[2,1,1280]{2,1,0:T(2,128)(2,1)}, bf16[2,1,1280]{2,1,0:T(2,128)(2,1)S(1)}, u32[]{:S(2)}) copy-start(bf16[2,1,1280]{2,1,0:T(2,128)(2,1)S(1)} %all-gather.1) | copy-start | bytes 15364
  370.8 93.7 %copy-start.47 = (bf16[128,1280]{1,0:T(8,128)(2,1)}, bf16[128,1280]{1,0:T(8,128)(2,1)S(1)}, u32[]{:S(2)}) copy-start(bf16[128,1280]{1,0:T(8,128)(2,1)S(1)} %fusion.26) | copy-start | bytes 983044
  375.1 216.6 %copy-start.62 = (bf16[2,1,1280]{2,1,0:T(2,128)(2,1)}, bf16[2,1,1280]{2,1,0:T(2,128)(2,1)S(1)}, u32[]{:S(2)}) copy-start(bf16[2,1,1280]{2,1,0:T(2,128)(2,1)S(1)} %all-gather) | copy-start | bytes 15364
  662.5 241.1 %reduce-scatter.11.cloned.1.call-start = ((), (), s32[]{:S(2)}) async-start(), calls=%async_computation.13 | async-start | bytes 3481600 | tf_op jit(solution)/shard_map/reduce_scatter | solution.py:269
  755.8 231.0 %reduce-scatter.9.cloned.1.call-start = ((), (), s32[]{:S(2)}) async-start(), calls=%async_computation.12 | async-start | bytes 10444800 | tf_op jit(solution)/shard_map/reduce_scatter | solution.py:266
  805.7 323.3 %reduce-scatter.13.cloned.1.call-start = ((), (), s32[]{:S(2)}) async-start(), calls=%async_computation.14 | async-start | bytes 13926400 | tf_op jit(solution)/shard_map/reduce_scatter | solution.py:272
  835.2 435.9 %reduce-scatter.15.cloned.1.call-start = ((), (), s32[]{:S(2)}) async-start(), calls=%async_computation.15 | async-start | bytes 13926400 | tf_op jit(solution)/shard_map/reduce_scatter | solution.py:275
  865.4 547.1 %reduce-scatter.17.cloned.1.call-start = ((), (), s32[]{:S(2)}) async-start(), calls=%async_computation.16 | async-start | bytes 13926400 | tf_op jit(solution)/shard_map/reduce_scatter | solution.py:287
  899.8 633.9 %all-reduce.19.cloned.1.call-start = ((), (), s32[]{:S(2)}) async-start(), calls=%async_computation.18 | async-start | bytes 9175040 | tf_op jit(solution)/shard_map/psum | solution.py:309
  1419.9 76.4 %copy-start.46 = (bf16[128,1280]{1,0:T(8,128)(2,1)S(1)}, bf16[128,1280]{1,0:T(8,128)(2,1)}, u32[]{:S(2)}) copy-start(bf16[128,1280]{1,0:T(8,128)(2,1)} %copy-done.45) | copy-start | bytes 983044
  1419.9 76.4 %copy-start.48 = (bf16[128,1280]{1,0:T(8,128)(2,1)S(1)}, bf16[128,1280]{1,0:T(8,128)(2,1)}, u32[]{:S(2)}) copy-start(bf16[128,1280]{1,0:T(8,128)(2,1)} %copy-done.47) | copy-start | bytes 983044
  1419.9 77.3 %copy-start.18 = (f32[128,1280]{1,0:T(8,128)S(1)}, f32[128,1280]{1,0:T(8,128)}, u32[]{:S(2)}) copy-start(f32[128,1280]{1,0:T(8,128)} %copy-done.17) | copy-start | bytes 1966084
  1419.9 77.2 %copy-start.20 = (f32[128,1280]{1,0:T(8,128)S(1)}, f32[128,1280]{1,0:T(8,128)}, u32[]{:S(2)}) copy-start(f32[128,1280]{1,0:T(8,128)} %copy-done.19) | copy-start | bytes 1966084
  (89 other events, 984.1 us)
Sparse Core Ops, SparseCore 0:
  10.4 87.1 all-gather.8
  99.9 44.1 all-gather.10
  146.4 102.8 all-gather.12
  251.4 102.1 all-gather.14
  355.7 102.1 all-gather.16
  460.1 102.1 all-gather.18
  662.6 136.5 reduce-scatter.18
  803.4 65.9 reduce-scatter.10
  873.6 113.2 reduce-scatter.8
  990.8 138.1 reduce-scatter.12
  1133.6 137.4 reduce-scatter.14
  1275.1 137.4 reduce-scatter.16
  1416.4 117.3 all-reduce.18
where the time goes:
time: 1560 us; the launch traced here: 1550 us
  waiting for transfers between devices  969 us (62%)
  matrix products  339 us (22%)
  blocking collectives  147 us (9%)
  local copies, waits for them, and re-layouts  41 us (3%)
  other arithmetic  33.2 us (2%)
  between operations  18 us (1%)
    reduce_scatter x1, waiting for transfers between devices, shards(): lax.psum_scatter(totals[3].astype(jnp.bfloat16), 'dp', scatter_dimension=...  142 us
    reduce_scatter x1, waiting for transfers between devices, shards(): lax.psum_scatter(totals[2].astype(jnp.bfloat16), 'dp', scatter_dimension=...  142 us
    reduce_scatter x1, waiting for transfers between devices, shards(): lax.psum_scatter(totals[7].astype(jnp.bfloat16), 'dp', scatter_dimension=...  141 us
    unnamed x3, blocking collectives  133 us
    dot_general x10, matrix products, row_product(): lax.dot_general(left, right, (((0,), (0,)), ((), ())), preferred_element_...  110 us
    all_gather x1, waiting for transfers between devices, shards(): lax.all_gather(up_weight, 'dp', axis=0, tiled=True)  98.3 us
    all_gather x1, waiting for transfers between devices, shards(): lax.all_gather(gene_weight, 'dp', axis=0, tiled=True)  97.8 us
    all_gather x1, waiting for transfers between devices, shards(): lax.all_gather(down_weight, 'dp', axis=0, tiled=True)  96.1 us
  transfers between devices with their start and end apart: 13, of which 11 were waited for; matrix products, arithmetic and copies ran while one was open for 19% of the time, Pallas kernels for 0%

commit v1 on v0

--- a/solution.py
+++ b/solution.py
@@ -8,6 +8,28 @@
 HEAD = 64
 highest = lax.Precision.HIGHEST
 epsilon = 1e-05
+
+
+def in_order(tiles, dim):
+    lengths = list(tiles.shape[1:])
+    lengths[dim] *= tiles.shape[0]
+    return jnp.moveaxis(tiles, 0, dim).reshape(lengths)
+
+
+def gather_around(value, axis, dim):
+    size = lax.axis_size(axis)
+    pairs = [(i, (i + 1) % size) for i in range(size)]
+    back = [(b, a) for a, b in pairs]
+    lower, upper = ([], [])
+    for step in range(size - 1):
+        if step % 2 == 0:
+            lower.append(lax.ppermute(lower[-1] if lower else value, axis, pairs))
+        else:
+            upper.append(lax.ppermute(upper[-1] if upper else value, axis, back))
+    tiles = jnp.stack([*lower[::-1], value, *upper])
+    shift = lax.axis_index(axis) - len(lower)
+    tiles = tiles[(jnp.arange(size) - shift) % size]
+    return in_order(tiles, dim)
 
 
 def row_product(left, right):
@@ -226,7 +248,7 @@
             lax.all_gather(attn_gain, "dp", axis=0, tiled=True),
             lax.all_gather(ffn_gain, "dp", axis=0, tiled=True),
             lax.all_gather(up_bias, "dp", axis=0, tiled=True),
-            lax.all_gather(cell_weight, "dp", axis=0, tiled=True),
+            gather_around(cell_weight, "dp", 0),
             lax.all_gather(gene_weight, "dp", axis=0, tiled=True),
             lax.all_gather(decoder_bias, "dp", axis=0, tiled=True),
             lax.all_gather(readout, "dp", axis=0, tiled=True),

time: 1560 us -> 1510 us (0.968)
  waiting for transfers between devices: 969 us -> 863 us
  local copies, waits for them, and re-layouts: 41 us -> 73.8 us
  starting transfers between devices: 1.09 us -> 33.3 us
    ppermute x0 -> x15, waiting for transfers between devices: none -> 138 us  [the longest x8 112 us: gather_around(): lower.append(lax.ppermute(lower[-1] if lower else value, axis, pairs))]
    all_gather x1, waiting for transfers between devices: 98.3 us -> 5.91 us  [shards(): lax.all_gather(up_weight, 'dp', axis=0, tiled=True)]
    all_gather x1 -> x0, waiting for transfers between devices: 82.8 us -> none  [shards(): lax.all_gather(cell_weight, 'dp', axis=0, tiled=True)]
    ppermute x0 -> x15, starting transfers between devices: none -> 32.4 us  [the longest x7 19 us: gather_around(): upper.append(lax.ppermute(upper[-1] if upper else value, axis, back))]
    all_gather x1, waiting for transfers between devices: 31.2 us -> 0.02 us  [shards(): lax.all_gather(out_weight, 'dp', axis=0, tiled=True)]
    all_gather x1, waiting for transfers between devices: 97.8 us -> 72.8 us  [shards(): lax.all_gather(gene_weight, 'dp', axis=0, tiled=True)]
    unnamed x222 -> x247, local copies, waits for them, and re-layouts: 34.9 us -> 54.6 us
    all_gather x1, waiting for transfers between devices: 16.6 us -> 0.01 us  [shards(): lax.all_gather(qkv_weight, 'dp', axis=0, tiled=True)]
  transfers between devices with their start and end apart: 13 -> 27, of which waited for: 11 -> 17; matrix products, arithmetic and copies ran while one was open for 19% -> 22% of each run, Pallas kernels for 0% -> 0%
where the time goes in v1:
time: 1510 us; the launch traced here: 1500 us
  waiting for transfers between devices  863 us (57%)
  matrix products  332 us (22%)
  blocking collectives  149 us (10%)
  local copies, waits for them, and re-layouts  73.8 us (5%)
  starting transfers between devices  33.3 us (2%)
  other arithmetic  33.2 us (2%)
  between operations  18.7 us (1%)
    reduce_scatter x1, waiting for transfers between devices, shards(): lax.psum_scatter(totals[7].astype(jnp.bfloat16), 'dp', scatter_dimension=...  142 us
    reduce_scatter x1, waiting for transfers between devices, shards(): lax.psum_scatter(totals[3].astype(jnp.bfloat16), 'dp', scatter_dimension=...  142 us
    reduce_scatter x1, waiting for transfers between devices, shards(): lax.psum_scatter(totals[2].astype(jnp.bfloat16), 'dp', scatter_dimension=...  142 us
    unnamed x3, blocking collectives  135 us
    dot_general x10, matrix products, row_product(): lax.dot_general(left, right, (((0,), (0,)), ((), ())), preferred_element_...  112 us
    ppermute x8, waiting for transfers between devices, gather_around(): lower.append(lax.ppermute(lower[-1] if lower else value, axis, pairs))  112 us
    all_gather x1, waiting for transfers between devices, shards(): lax.all_gather(down_weight, 'dp', axis=0, tiled=True)  101 us
    reduce_scatter x1, waiting for transfers between devices, shards(): lax.psum_scatter(totals[0].astype(jnp.bfloat16), 'dp', scatter_dimension=...  82.7 us
  transfers between devices with their start and end apart: 27, of which 17 were waited for; matrix products, arithmetic and copies ran while one was open for 22% of the time, Pallas kernels for 0%

profile of v1, /device:TPU:0, one launch (start us, length us, event | category | flops | bytes accessed | tf_op | source)
XLA Modules:
  0.0 1502.6 jit_solution(4156774575122488580)
XLA Ops:
  10.6 15.4 %collective-permute-done = bf16[80,5120]{1,0:T(8,128)(2,1)S(1)} collective-permute-done((bf16[80,5120]{1,0:T(8,128)(2,1)}, bf16[80,5120]{1,0:T(8,128)(2,1)S(1)}, u32[]{:S(2)}, u32[]{:S(2)}) %collective-permute-start) | collective-permute-done | bytes 819232 | tf_op jit(solution)/shard_map/ppermute | solution.py:26
  30.4 25.2 %collective-permute-done.1 = bf16[80,5120]{1,0:T(8,128)(2,1)S(1)} collective-permute-done((bf16[80,5120]{1,0:T(8,128)(2,1)S(1)}, bf16[80,5120]{1,0:T(8,128)(2,1)S(1)}, u32[]{:S(2)}, u32[]{:S(2)}) %collective-permute-start.1) | collective-permute-done | bytes 819232 | tf_op jit(solution)/shard_map/ppermute | solution.py:26
  60.1 26.3 %collective-permute-done.2 = bf16[80,5120]{1,0:T(8,128)(2,1)S(1)} collective-permute-done((bf16[80,5120]{1,0:T(8,128)(2,1)S(1)}, bf16[80,5120]{1,0:T(8,128)(2,1)S(1)}, u32[]{:S(2)}, u32[]{:S(2)}) %collective-permute-start.2) | collective-permute-done | bytes 819232 | tf_op jit(solution)/shard_map/ppermute | solution.py:26
  106.9 13.0 collective-permute-done.4
  128.9 20.5 %collective-permute-done.5 = bf16[80,5120]{1,0:T(8,128)(2,1)} collective-permute-done((bf16[80,5120]{1,0:T(8,128)(2,1)S(1)}, bf16[80,5120]{1,0:T(8,128)(2,1)}, u32[]{:S(2)}, u32[]{:S(2)}) %collective-permute-start.5) | collective-permute-done | bytes 819232 | tf_op jit(solution)/shard_map/ppermute | solution.py:26
  152.6 66.8 %all-reduce.13 = (bf16[1280]{0:T(1024)(128)(2,1)S(1)}, bf16[5120]{0:T(1024)(128)(2,1)S(1)}, bf16[1280]{0:T(1024)(128)(2,1)S(1)}, bf16[5120]{0:T(1024)(128)(2,1)S(1)}, bf16[5120]{0:T(1024)(128)(2,1)S(1)}) all-reduce(bf16[1280]{0:T(1024)(128)(2,1)S(1)} %dynamic-update-slice.6, ...), channel_id=1, replica_groups=mesh['dp'=16,'query'=2] {'dp'}, use_global_device_ids=true, to_apply=%add | all-reduce | flops 17920 | bytes 71680
  221.3 22.9 %collective-permute-done.13 = bf16[80,5120]{1,0:T(8,128)(2,1)S(1)} collective-permute-done((bf16[80,5120]{1,0:T(8,128)(2,1)}, bf16[80,5120]{1,0:T(8,128)(2,1)S(1)}, u32[]{:S(2)}, u32[]{:S(2)}) %collective-permute-start.13) | collective-permute-done | bytes 819232 | tf_op jit(solution)/shard_map/ppermute | solution.py:28
  322.5 101.2 %all-gather.14.cloned.1.call-done = bf16[5120,1280]{1,0:T(8,128)(2,1)} async-done(((bf16[320,1280]{1,0:T(8,128)(2,1)}), bf16[5120,1280]{1,0:T(8,128)(2,1)}) %all-gather.14.cloned.1.call-update) | async-done | bytes 13107216 | tf_op jit(solution)/shard_map/all_gather | solution.py:247
  455.2 72.8 %all-gather.16.cloned.1.call-done = bf16[1280,5120]{1,0:T(8,128)(2,1)} async-done(((bf16[80,5120]{1,0:T(8,128)(2,1)}), bf16[1280,5120]{1,0:T(8,128)(2,1)}) %all-gather.16.cloned.1.call-update) | async-done | bytes 13107216 | tf_op jit(solution)/shard_map/all_gather | solution.py:252
  581.6 16.2 %fusion.2 = bf16[1280,5120]{0,1:T(8,128)(2,1)} fusion(f32[5120,1280]{1,0:T(8,128)} %fusion.51, bf16[384,5120]{1,0:T(8,128)(2,1)} %get-tuple-element.137, bf16[2,1,384,1280]{3,2,1,0:T(8,128)(2,1)} %param.34), kind=kOutput, calls=%fused_computation.8 | convolution fusion | flops 5046272000 | bytes 44236800 | tf_op jit(solution)/shard_map/dot_general | solution.py:36
  597.8 17.6 %copy.89 = bf16[1280,5120]{1,0:T(8,128)(2,1)} copy(bf16[1280,5120]{0,1:T(8,128)(2,1)} %fusion.2) | data formatting | bytes 26214400
  623.3 14.1 convolution_convert_fusion.5
  637.5 13.5 convolution_convert_fusion.4
  759.0 13.9 fusion.167
  772.9 18.1 %add_convert_fusion.1 = bf16[1280,5120]{1,0:T(8,128)(2,1)} fusion(f32[1280,5120]{1,0:T(8,128)} %fusion.167, f32[2,5120]{1,0:T(2,128)S(1)} %fusion.134, bf16[2,1,1280]{2,1,0:T(2,128)(2,1)S(1)} %copy-done.75), kind=kOutput, calls=%fused_computation.4 | convolution fusion | flops 170393600 | bytes 39367680 | tf_op jit(solution)/shard_map/dot_general | solution.py:210
  804.7 15.9 %add_convert_fusion.2 = bf16[5120,1280]{1,0:T(8,128)(2,1)} fusion(f32[5120,1280]{1,0:T(8,128)} %fusion.146, f32[128,1280]{1,0:T(8,128)S(1)} %copy-done.22, f32[128,5120]{1,0:T(8,128)} %copy-done.11), kind=kOutput, calls=%fused_computation.5 | convolution fusion | flops 1696890880 | bytes 42598400 | tf_op jit(solution)/shard_map/dot_general | solution.py:36
  821.7 12.8 fusion.187
  834.5 18.8 %add_convert_fusion.3 = bf16[1280,5120]{1,0:T(8,128)(2,1)} fusion(f32[1280,5120]{1,0:T(8,128)} %fusion.187, bf16[128,5120]{1,0:T(8,128)(2,1)} %copy-done.26, f32[128,1280]{1,0:T(8,128)S(1)} %copy-done.6, f32[128]{0:T(128)S(1)} %add_rsqrt_fusion, f32[128]{0:T(128)S(1)} %broadcast_multiply_fusion.8, f32[1280]{0:T(1024)S(1)} %convert_element_type.331), kind=kOutput, calls=%fused_computation.6 | convolution fusion | flops 1691484160 | bytes 41293824 | tf_op jit(solution)/shard_map/dot_general | solution.py:36
  857.0 82.7 %reduce-scatter.9.cloned.1.call-done = bf16[80,3840]{1,0:T(8,128)(2,1)} async-done(((bf16[1280,3840]{1,0:T(8,128)(2,1)}), bf16[80,3840]{1,0:T(8,128)(2,1)}) %reduce-scatter.9.cloned.1.call-update) | async-done | bytes 614416 | tf_op jit(solution)/shard_map/reduce_scatter | solution.py:288
  939.8 142.3 %reduce-scatter.17.cloned.1.call-done = bf16[80,5120]{1,0:T(8,128)(2,1)} async-done(((bf16[1280,5120]{1,0:T(8,128)(2,1)}), bf16[80,5120]{1,0:T(8,128)(2,1)}) %reduce-scatter.17.cloned.1.call-update) | async-done | bytes 819216 | tf_op jit(solution)/shard_map/reduce_scatter | solution.py:309
  1082.1 142.1 %reduce-scatter.15.cloned.1.call-done = bf16[320,1280]{1,0:T(8,128)(2,1)} async-done(((bf16[5120,1280]{1,0:T(8,128)(2,1)}), bf16[320,1280]{1,0:T(8,128)(2,1)}) %reduce-scatter.15.cloned.1.call-update) | async-done | bytes 819216 | tf_op jit(solution)/shard_map/reduce_scatter | solution.py:297
  1224.2 141.6 %reduce-scatter.13.cloned.1.call-done = bf16[80,5120]{1,0:T(8,128)(2,1)} async-done(((bf16[1280,5120]{1,0:T(8,128)(2,1)}), bf16[80,5120]{1,0:T(8,128)(2,1)}) %reduce-scatter.13.cloned.1.call-update) | async-done | bytes 819216 | tf_op jit(solution)/shard_map/reduce_scatter | solution.py:294
  1381.6 59.7 %all-reduce.12 = (bf16[1280]{0:T(1024)(128)(2,1)S(1)}, bf16[1280]{0:T(1024)(128)(2,1)S(1)}, bf16[5120]{0:T(1024)(128)(2,1)S(1)}, bf16[5120]{0:T(1024)(128)(2,1)S(1)}, bf16[5120]{0:T(1024)(128)(2,1)S(1)}) all-reduce(bf16[1280]{0:T(1024)(128)(2,1)S(1)} %add_convert_fusion.9, ...), channel_id=8, replica_groups=mesh['dp'=16,'query'=2] {'dp'}, use_global_device_ids=true, to_apply=%region_36.37.clone | all-reduce | flops 17920 | bytes 71680
  1453.1 33.7 %all-reduce.19.cloned.1.call-done = (bf16[80,5120]{0,1:T(8,128)(2,1)}, bf16[80,3840]{1,0:T(8,128)(2,1)}, bf16[80,1280]{1,0:T(8,128)(2,1)}, bf16[80,5120]{1,0:T(8...) async-done(((bf16[80,5120]{0,1:T(8,128)(2,1)}, bf16[80,3840]{1,0:T(8,128)(2,1)}, bf16[80,1280]{1,0:T(8,128)(2,1)}, bf16[80,5120]{1,0:T(8,128)(2,1)}, ...) | async-done | bytes 4096016 | tf_op jit(solution)/shard_map/psum | solution.py:331
  (414 shorter events, 376.9 us)
Async XLA Ops:
  7.3 277.1 %all-gather.8.cloned.1.call-start = ((), (), s32[]{:S(2)}) async-start(), calls=%async_computation.6 | async-start | bytes 10444800 | tf_op jit(solution)/shard_map/all_gather | solution.py:244
  8.0 293.4 %all-gather.10.cloned.1.call-start = ((), (), s32[]{:S(2)}) async-start(), calls=%async_computation.7 | async-start | bytes 3481600 | tf_op jit(solution)/shard_map/all_gather | solution.py:245
  8.8 305.5 %all-gather.12.cloned.1.call-start = ((), (), s32[]{:S(2)}) async-start(), calls=%async_computation.8 | async-start | bytes 13926400 | tf_op jit(solution)/shard_map/all_gather | solution.py:246
  9.5 414.2 %all-gather.14.cloned.1.call-start = ((), (), s32[]{:S(2)}) async-start(), calls=%async_computation.9 | async-start | bytes 13926400 | tf_op jit(solution)/shard_map/all_gather | solution.py:247
  10.1 517.9 %all-gather.16.cloned.1.call-start = ((), (), s32[]{:S(2)}) async-start(), calls=%async_computation.10 | async-start | bytes 13926400 | tf_op jit(solution)/shard_map/all_gather | solution.py:252
  26.0 29.6 %collective-permute-start.1 = (bf16[80,5120]{1,0:T(8,128)(2,1)S(1)}, bf16[80,5120]{1,0:T(8,128)(2,1)S(1)}, u32[]{:S(2)}, u32[]{:S(2)}) collective-permute-start(bf16[80,5120]{1,0:T(8,128)(2,1)S(1)} %collective-permute-done), channel_id=1, source_target_pairs={{0,2},{2,4},{4,6},{6,8},{8,10},{10,12},{12,14},{14,16},{16,18},{18... | collective-permute-start | bytes 2457608 | tf_op jit(solution)/shard_map/ppermute | solution.py:26
  26.0 29.6 %collective-permute-start.8 = (bf16[80,5120]{1,0:T(8,128)(2,1)}, bf16[80,5120]{1,0:T(8,128)(2,1)S(1)}, u32[]{:S(2)}, u32[]{:S(2)}) collective-permute-start(bf16[80,5120]{1,0:T(8,128)(2,1)} %param.30), channel_id=1, source_target_pairs={{2,0},{4,2},{6,4},{8,6},{10,8},{12,10},{14,12},{16,14},{18,16},{20... | collective-permute-start | bytes 2457608 | tf_op jit(solution)/shard_map/ppermute | solution.py:28
  55.6 30.8 %collective-permute-start.2 = (bf16[80,5120]{1,0:T(8,128)(2,1)S(1)}, bf16[80,5120]{1,0:T(8,128)(2,1)S(1)}, u32[]{:S(2)}, u32[]{:S(2)}) collective-permute-start(bf16[80,5120]{1,0:T(8,128)(2,1)S(1)} %collective-permute-done.1), channel_id=1, source_target_pairs={{0,2},{2,4},{4,6},{6,8},{8,10},{10,12},{12,14},{14,16},{16,18},{18... | collective-permute-start | bytes 2457608 | tf_op jit(solution)/shard_map/ppermute | solution.py:26
  55.7 30.8 %collective-permute-start.9 = (bf16[80,5120]{1,0:T(8,128)(2,1)S(1)}, bf16[80,5120]{1,0:T(8,128)(2,1)S(1)}, u32[]{:S(2)}, u32[]{:S(2)}) collective-permute-start(bf16[80,5120]{1,0:T(8,128)(2,1)S(1)} %collective-permute-done.8), channel_id=1, source_target_pairs={{2,0},{4,2},{6,4},{8,6},{10,8},{12,10},{14,12},{16,14},{18,16},{20... | collective-permute-start | bytes 2457608 | tf_op jit(solution)/shard_map/ppermute | solution.py:28
  86.4 19.6 %collective-permute-start.10 = (bf16[80,5120]{1,0:T(8,128)(2,1)S(1)}, bf16[80,5120]{1,0:T(8,128)(2,1)S(1)}, u32[]{:S(2)}, u32[]{:S(2)}) collective-permute-start(bf16[80,5120]{1,0:T(8,128)(2,1)S(1)} %collective-permute-done.9), channel_id=1, source_target_pairs={{2,0},{4,2},{6,4},{8,6},{10,8},{12,10},{14,12},{16,14},{18,16},{20... | collective-permute-start | bytes 2457608 | tf_op jit(solution)/shard_map/ppermute | solution.py:28
  106.0 22.3 %collective-permute-start.11 = (bf16[80,5120]{1,0:T(8,128)(2,1)S(1)}, bf16[80,5120]{1,0:T(8,128)(2,1)}, u32[]{:S(2)}, u32[]{:S(2)}) collective-permute-start(bf16[80,5120]{1,0:T(8,128)(2,1)S(1)} %collective-permute-done.10), channel_id=1, source_target_pairs={{2,0},{4,2},{6,4},{8,6},{10,8},{12,10},{14,12},{16,14},{18,16},{20... | collective-permute-start | bytes 2457608 | tf_op jit(solution)/shard_map/ppermute | solution.py:28
  120.0 29.4 %collective-permute-start.5 = (bf16[80,5120]{1,0:T(8,128)(2,1)S(1)}, bf16[80,5120]{1,0:T(8,128)(2,1)}, u32[]{:S(2)}, u32[]{:S(2)}) collective-permute-start(bf16[80,5120]{1,0:T(8,128)(2,1)S(1)} %collective-permute-done.4), channel_id=1, source_target_pairs={{0,2},{2,4},{4,6},{6,8},{8,10},{10,12},{12,14},{14,16},{16,18},{18... | collective-permute-start | bytes 2457608 | tf_op jit(solution)/shard_map/ppermute | solution.py:26
  128.4 91.9 %collective-permute-start.12 = (bf16[80,5120]{1,0:T(8,128)(2,1)}, bf16[80,5120]{1,0:T(8,128)(2,1)}, u32[]{:S(2)}, u32[]{:S(2)}) collective-permute-start(bf16[80,5120]{1,0:T(8,128)(2,1)} %collective-permute-done.11), channel_id=1, source_target_pairs={{2,0},{4,2},{6,4},{8,6},{10,8},{12,10},{14,12},{16,14},{18,16},{20... | collective-permute-start | bytes 2457608 | tf_op jit(solution)/shard_map/ppermute | solution.py:28
  149.3 71.0 %collective-permute-start.6 = (bf16[80,5120]{1,0:T(8,128)(2,1)}, bf16[80,5120]{1,0:T(8,128)(2,1)}, u32[]{:S(2)}, u32[]{:S(2)}) collective-permute-start(bf16[80,5120]{1,0:T(8,128)(2,1)} %collective-permute-done.5), channel_id=1, source_target_pairs={{0,2},{2,4},{4,6},{6,8},{8,10},{10,12},{12,14},{14,16},{16,18},{18... | collective-permute-start | bytes 2457608 | tf_op jit(solution)/shard_map/ppermute | solution.py:26
  149.4 705.3 %reduce-scatter.19.cloned.1.call-start = ((), (), s32[]{:S(2)}) async-start(), calls=%async_computation.16 | async-start | bytes 13926400
  220.3 23.8 %collective-permute-start.13 = (bf16[80,5120]{1,0:T(8,128)(2,1)}, bf16[80,5120]{1,0:T(8,128)(2,1)S(1)}, u32[]{:S(2)}, u32[]{:S(2)}) collective-permute-start(bf16[80,5120]{1,0:T(8,128)(2,1)} %collective-permute-done.12), channel_id=1, source_target_pairs={{2,0},{4,2},{6,4},{8,6},{10,8},{12,10},{14,12},{16,14},{18,16},{20... | collective-permute-start | bytes 2457608 | tf_op jit(solution)/shard_map/ppermute | solution.py:28
  220.4 28.6 %collective-permute-start.7 = (bf16[80,5120]{1,0:T(8,128)(2,1)}, bf16[80,5120]{1,0:T(8,128)(2,1)S(1)}, u32[]{:S(2)}, u32[]{:S(2)}) collective-permute-start(bf16[80,5120]{1,0:T(8,128)(2,1)} %collective-permute-done.6), channel_id=1, source_target_pairs={{0,2},{2,4},{4,6},{6,8},{8,10},{10,12},{12,14},{14,16},{16,18},{18... | collective-permute-start | bytes 2457608 | tf_op jit(solution)/shard_map/ppermute | solution.py:26
  244.1 27.5 %collective-permute-start.14 = (bf16[80,5120]{1,0:T(8,128)(2,1)S(1)}, bf16[80,5120]{1,0:T(8,128)(2,1)S(1)}, u32[]{:S(2)}, u32[]{:S(2)}) collective-permute-start(bf16[80,5120]{1,0:T(8,128)(2,1)S(1)} %collective-permute-done.13), channel_id=1, source_target_pairs={{2,0},{4,2},{6,4},{8,6},{10,8},{12,10},{14,12},{16,14},{18,16},{20... | collective-permute-start | bytes 2457608 | tf_op jit(solution)/shard_map/ppermute | solution.py:28
  615.4 241.7 %reduce-scatter.11.cloned.1.call-start = ((), (), s32[]{:S(2)}) async-start(), calls=%async_computation.12 | async-start | bytes 3481600 | tf_op jit(solution)/shard_map/reduce_scatter | solution.py:291
  708.4 231.4 %reduce-scatter.9.cloned.1.call-start = ((), (), s32[]{:S(2)}) async-start(), calls=%async_computation.11 | async-start | bytes 10444800 | tf_op jit(solution)/shard_map/reduce_scatter | solution.py:288
  758.4 323.7 %reduce-scatter.17.cloned.1.call-start = ((), (), s32[]{:S(2)}) async-start(), calls=%async_computation.15 | async-start | bytes 13926400 | tf_op jit(solution)/shard_map/reduce_scatter | solution.py:309
  791.0 433.1 %reduce-scatter.15.cloned.1.call-start = ((), (), s32[]{:S(2)}) async-start(), calls=%async_computation.14 | async-start | bytes 13926400 | tf_op jit(solution)/shard_map/reduce_scatter | solution.py:297
  820.6 545.2 %reduce-scatter.13.cloned.1.call-start = ((), (), s32[]{:S(2)}) async-start(), calls=%async_computation.13 | async-start | bytes 13926400 | tf_op jit(solution)/shard_map/reduce_scatter | solution.py:294
  853.3 633.5 %all-reduce.19.cloned.1.call-start = ((), (), s32[]{:S(2)}) async-start(), calls=%async_computation.17 | async-start | bytes 9175040 | tf_op jit(solution)/shard_map/psum | solution.py:331
  (108 other events, 3994.1 us)
Sparse Core Ops, SparseCore 0:
  10.4 132.1 all-gather.7
  144.9 53.4 all-gather.9
  200.7 113.5 all-gather.11
  316.4 107.2 all-gather.13
  425.8 102.1 all-gather.15
  615.5 136.5 reduce-scatter.18
  756.4 65.9 reduce-scatter.10
  826.5 113.2 reduce-scatter.8
  943.9 138.1 reduce-scatter.16
  1086.6 137.5 reduce-scatter.14
  1228.3 137.4 reduce-scatter.12
  1369.5 117.2 all-reduce.18
